TPU v7x, 512 devices: a whole 4x8x8 slice. The times are simulated.
512 devices in a mesh: dp: 16 (over z, core), seq: 32 (over x, y).
Axes of the slice: x: 4, y: 8, z: 8, core: 2. Of those that a mesh axis runs over, the one named last changes fastest.
Arguments:
- inputs: bfloat16 [16, 4096, 4096], P('dp', 'seq'), may hold values from -6 to 6
- out_grads: bfloat16 [16, 4096, 14336], P('dp', 'seq'), may hold values from -6 to 6
- valid: int32 [16, 4096], P('dp', 'seq'), may hold values 0 or 1
- doc_blocks: int32 [16, 4], P('dp'), may hold values from 1 to 16, 32 in all within a row
- doc_ids: int32 [64], replicated, may hold values from 0 to 63, each once
- proj_in: bfloat16 [4096, 64], P('seq'), may hold values from -0.09375 to 0.09375
- proj_out: bfloat16 [14336, 64], P('seq'), may hold values from -0.046875 to 0.046875
- test_grads: bfloat16 [1024, 4096], P('seq'), may hold values from -192 to 192
Outputs:
- scores: float32 [64, 1024], P(None, 'seq')
Inputs may be any that keep to these rules, and one draw needn't show every extreme that they name: `doc_blocks`: each group's lengths sum to 32; the largest is 16 in every group. `doc_ids`: every document number appears once.
All inputs are finite; a program needn't handle non-finite values. No bound on the sum of `valid` on one device may be relied on, other than what follows from the above.
Results may differ from a plain program's by a relative error of at most 0.0003.
Values may be sent and summed in bfloat16 or wider, within the bound.
A program may use at most 64 MiB of HBM per device.

v0:
```python
import jax
import jax.numpy as jnp
from jax import lax
from jax.sharding import PartitionSpec as P

PROJ_OUT = 64
FEAT = 4096
BLOCK = 128
DOC_GRP = 4


def per_device(inputs, out_grads, valid, doc_blocks, doc_ids, proj_in, proj_out, test_grads):
    tokens = inputs[0]
    outgrad = out_grads[0]
    slots = tokens.shape[0]
    columns = tokens
    px = jnp.dot(
        columns,
        lax.all_gather(proj_in, "seq", axis=0, tiled=True),
        preferred_element_type=jnp.float32,
    )
    columns = outgrad
    pg = jnp.dot(
        columns,
        lax.all_gather(proj_out, "seq", axis=0, tiled=True),
        preferred_element_type=jnp.float32,
    )
    ends = jnp.cumsum(doc_blocks[0])
    position = lax.axis_index("seq") * slots + jnp.arange(slots, dtype=jnp.int32)
    blk = position // BLOCK
    owner = jnp.sum((blk[:, None] >= ends[None, :]).astype(jnp.int32), axis=1)
    onehot = (
        (owner[:, None] == jnp.arange(DOC_GRP, dtype=jnp.int32)[None, :]) & (valid[0][:, None] == 1)
    ).astype(jnp.float32)
    weighted = (onehot[:, :, None] * pg[:, None, :]).reshape(slots, DOC_GRP * PROJ_OUT)
    partial_grads = jnp.dot(weighted.T, px, precision=lax.Precision.HIGHEST).reshape(DOC_GRP, FEAT)
    ndocs = DOC_GRP * lax.axis_size("dp")
    group_grads = lax.psum(partial_grads, "seq")
    doc_grads = lax.all_gather(group_grads, "dp", axis=0, tiled=True)
    gram = jnp.dot(doc_grads, doc_grads.T, precision=lax.Precision.HIGHEST)
    cross = jnp.dot(doc_grads, test_grads.astype(jnp.float32).T, precision=lax.Precision.HIGHEST)
    damp = 0.1 * jnp.trace(gram) / ndocs
    matrix = gram / ndocs + damp * jnp.eye(ndocs, dtype=jnp.float32)
    factor = jnp.linalg.cholesky(matrix)
    middle = lax.linalg.triangular_solve(factor, cross, left_side=True, lower=True)
    solved = lax.linalg.triangular_solve(
        factor, middle, left_side=True, lower=True, transpose_a=True
    )
    placing = (doc_ids[None, :] == jnp.arange(ndocs, dtype=jnp.int32)[:, None]).astype(jnp.float32)
    return jnp.dot(placing, solved, precision=lax.Precision.HIGHEST)


def solution(mesh):
    in_specs = (
        P("dp", "seq", None),
        P("dp", "seq", None),
        P("dp", "seq"),
        P("dp", None),
        P(),
        P("seq", None),
        P("seq", None),
        P("seq", None),
    )
    out_specs = P(None, "seq")
    return jax.shard_map(
        per_device, mesh=mesh, in_specs=in_specs, out_specs=out_specs, check_vma=False
    )
```

profile of v0, /device:TPU:1, one launch (start us, length us, event | category | flops | bytes accessed | tf_op | source)
XLA Modules:
  0.0 325.9 jit_solution(14330074124522014039)
XLA Ops:
  6.5 0.7 all-gather.5.cloned.1.call-update
  7.3 0.8 reduce-window.8
  8.1 0.1 convert_reduce_fusion
  8.2 41.4 %all_gather.10 = bf16[4096,64]{0,1:T(8,128)(2,1)S(1)} all-gather(bf16[128,64]{0,1:T(8,128)(2,1)} %param.13), channel_id=1, replica_groups=mesh['dp'=16,'seq'=32] {'seq'}, dimensions={0}, use_global_device_ids=true | all-gather | bytes 540672 | tf_op jit(solution)/shard_map/all_gather | solution.py:19
  49.6 0.7 compare_bitcast_fusion
  50.3 0.5 fusion.2
  50.8 44.7 %all-gather.5.cloned.1.call-done = bf16[32,448,64]{1,2,0:T(8,128)(2,1)} async-done(((bf16[1,448,64]{1,2,0:T(8,128)(2,1)}), bf16[32,448,64]{1,2,0:T(8,128)(2,1)}) %all-gather.5.cloned.1.call-update) | async-done | bytes 1835024 | tf_op jit(solution)/shard_map/all_gather | solution.py:25
  95.6 2.8 copy.20
  98.3 3.4 %reshape.113 = bf16[14336,64]{0,1:T(8,128)(2,1)} reshape(bf16[32,448,64]{1,0,2:T(8,128)(2,1)S(1)} %copy.20) | data formatting | bytes 3670016
  101.7 4.0 %fusion = f32[128,64]{0,1:T(8,128)S(1)} fusion(bf16[14336,64]{0,1:T(8,128)(2,1)} %reshape.113, bf16[1,128,14336]{2,1,0:T(8,128)(2,1)} %param.9), kind=kOutput, calls=%fused_computation | convolution fusion | flops 234881024 | bytes 5537792 | tf_op jit(solution)/shard_map/dot_general | solution.py:23
  105.7 0.3 fusion.15
  106.0 0.7 reshape.111
  106.8 147.6 %all-reduce.2.cloned.1.call-done = f32[4,4096]{1,0:T(4,128)} async-done(((f32[4,4096]{1,0:T(4,128)}), f32[4,4096]{1,0:T(4,128)}) %all-reduce.2.cloned.1.call-update) | async-done | bytes 65552 | tf_op jit(solution)/shard_map/psum | solution.py:38
  254.4 47.1 %all-gather.7.cloned.1.call-done = f32[16,4,4096]{2,1,0:T(4,128)} async-done(((f32[1,4,4096]{2,1,0:T(4,128)}), f32[16,4,4096]{2,1,0:T(4,128)}) %all-gather.7.cloned.1.call-update) | async-done | bytes 1048592 | tf_op jit(solution)/shard_map/all_gather | solution.py:39
  301.5 1.6 reshape.115
  303.1 1.6 select_reduce_fusion.1
  305.6 5.8 %cholesky.17 = f32[64,64]{1,0:T(8,128)S(1)} custom-call(f32[64,64]{1,0:T(8,128)S(1)} %fusion.10), custom_call_target="Cholesky" | custom-call | tf_op jit(solution)/shard_map/jit(cholesky)/cholesky | solution.py:44
  311.4 0.6 compare_reduce_fusion
  312.1 0.7 fusion.4
  312.8 4.9 %custom-call.8 = f32[1,64,64]{1,2,0:T(8,128)S(1)} custom-call(f32[1,64,64]{2,1,0:T(8,128)S(1)} %fusion.4), custom_call_target="InvertDiagBlocksLowerTriangular" | custom-call | tf_op jit(solution)/shard_map/triangular_solve | solution.py:46
  317.7 0.6 fusion.16
  318.3 0.1 fusion.7
  318.4 0.2 fusion.5
  318.6 0.8 fusion.11
  (19 shorter events, 0.4 us)
Async XLA Ops:
  6.5 43.8 %copy-start = (bf16[1,128,4096]{2,1,0:T(8,128)(2,1)S(1)}, bf16[1,128,4096]{2,1,0:T(8,128)(2,1)}, u32[]{:S(2)}) copy-start(bf16[1,128,4096]{2,1,0:T(8,128)(2,1)} %param.8) | copy-start | bytes 3145732
  6.5 89.0 %all-gather.5.cloned.1.call-start = ((), (), s32[]{:S(2)}) async-start(), calls=%async_computation.1 | async-start | bytes 2162688 | tf_op jit(solution)/shard_map/all_gather | solution.py:25
  7.3 247.2 %all-reduce.2.cloned.1.call-start = ((), (), s32[]{:S(2)}) async-start(), calls=%async_computation | async-start | bytes 131072 | tf_op jit(solution)/shard_map/psum | solution.py:38
  106.7 194.8 %all-gather.7.cloned.1.call-start = ((), (), s32[]{:S(2)}) async-start(), calls=%async_computation.2 | async-start | bytes 1114112 | tf_op jit(solution)/shard_map/all_gather | solution.py:39
  254.4 63.2 %copy-start.1 = (bf16[32,4096]{1,0:T(8,128)(2,1)S(1)}, bf16[32,4096]{1,0:T(8,128)(2,1)}, u32[]{:S(2)}) copy-start(bf16[32,4096]{1,0:T(8,128)(2,1)} %param.15) | copy-start | bytes 786436
  303.1 15.5 %copy-start.2 = (s32[64]{0:T(128)S(1)}, s32[64]{0:T(128)}, u32[]{:S(2)}) copy-start(s32[64]{0:T(128)} %param.12) | copy-start | bytes 772
Sparse Core Ops, SparseCore 0:
  10.5 84.9 all-gather.4
  106.8 147.5 all-reduce.1
  256.5 44.9 all-gather.6
where the time goes:
time: 326 us
  waiting for transfers between devices  240 us (74%)
  blocking collectives  41.4 us (13%)
  between operations  13.9 us (4%)
  other arithmetic  13.7 us (4%)
  local copies, waits for them, and re-layouts  8.61 us (3%)
  matrix products  8 us (2%)
    psum x1, waiting for transfers between devices, per_device(): group_grads = lax.psum(partial_grads, 'seq')  148 us
    all_gather x1, waiting for transfers between devices, per_device(): doc_grads = lax.all_gather(group_grads, 'dp', axis=0, tiled=True)  47.1 us
    all_gather x1, waiting for transfers between devices, per_device(): lax.all_gather(proj_out, 'seq', axis=0, tiled=True)  44.7 us
    all_gather x1, blocking collectives, per_device(): lax.all_gather(proj_in, 'seq', axis=0, tiled=True)  41.4 us
  transfers between devices with their start and end apart: 3, of which 3 were waited for; matrix products, arithmetic and copies ran while one was open for 1% of the time, Pallas kernels for 0%

commit v1 on v0

--- a/solution.py
+++ b/solution.py
@@ -9,16 +9,23 @@
 DOC_GRP = 4
 
 
+def process_the_rates(inp):
+    how_many = jax.lax.axis_size("seq")
+    block_list = []
+    for hop_no in [*range(inp.ndim)]:
+        block_list.append(how_many if hop_no == 0 else 1)
+    state_next = jax.lax.all_to_all(
+        jnp.tile(inp, block_list), "seq", split_axis=0, concat_axis=0, tiled=True
+    )
+    return state_next
+
+
 def per_device(inputs, out_grads, valid, doc_blocks, doc_ids, proj_in, proj_out, test_grads):
     tokens = inputs[0]
     outgrad = out_grads[0]
     slots = tokens.shape[0]
     columns = tokens
-    px = jnp.dot(
-        columns,
-        lax.all_gather(proj_in, "seq", axis=0, tiled=True),
-        preferred_element_type=jnp.float32,
-    )
+    px = jnp.dot(columns, process_the_rates(proj_in), preferred_element_type=jnp.float32)
     columns = outgrad
     pg = jnp.dot(
         columns,

time: 326 us -> 326 us (level)
  blocking collectives: 41.4 us -> 0 us
  waiting for transfers between devices: 240 us -> 270 us
  starting transfers between devices: 0.08 us -> 10.6 us
    all_gather x1 -> x0, blocking collectives: 41.4 us -> none  [per_device(): lax.all_gather(proj_in, 'seq', axis=0, tiled=True)]
    all_gather x1, waiting for transfers between devices: 44.7 us -> 61.4 us  [per_device(): lax.all_gather(proj_out, 'seq', axis=0, tiled=True)]
    all_to_all x0 -> x1, waiting for transfers between devices: none -> 12.7 us  [process_the_rates(): jax.lax.all_to_all(jnp.tile(inp, block_list), 'seq', split_axis=0, concat...]
    all_to_all x0 -> x1, starting transfers between devices: none -> 10.5 us  [process_the_rates(): jax.lax.all_to_all(jnp.tile(inp, block_list), 'seq', split_axis=0, concat...]
  transfers between devices with their start and end apart: 3 -> 4, of which waited for: 3 -> 4; matrix products, arithmetic and copies ran while one was open for 1% -> 1% of each run, Pallas kernels for 0% -> 0%
where the time goes in v1:
time: 326 us
  waiting for transfers between devices  270 us (83%)
  between operations  13.9 us (4%)
  other arithmetic  13.7 us (4%)
  starting transfers between devices  10.6 us (3%)
  local copies, waits for them, and re-layouts  10.2 us (3%)
  matrix products  7.98 us (2%)
    psum x1, waiting for transfers between devices, per_device(): group_grads = lax.psum(partial_grads, 'seq')  148 us
    all_gather x1, waiting for transfers between devices, per_device(): lax.all_gather(proj_out, 'seq', axis=0, tiled=True)  61.4 us
    all_gather x1, waiting for transfers between devices, per_device(): doc_grads = lax.all_gather(group_grads, 'dp', axis=0, tiled=True)  47.1 us
    all_to_all x1, waiting for transfers between devices, process_the_rates(): jax.lax.all_to_all(jnp.tile(inp, block_list), 'seq', split_axis=0, concat...  12.7 us
    all_to_all x1, starting transfers between devices, process_the_rates(): jax.lax.all_to_all(jnp.tile(inp, block_list), 'seq', split_axis=0, concat...  10.5 us
  transfers between devices with their start and end apart: 4, of which 4 were waited for; matrix products, arithmetic and copies ran while one was open for 1% of the time, Pallas kernels for 0%

profile of v1, /device:TPU:1, one launch (start us, length us, event | category | flops | bytes accessed | tf_op | source)
XLA Modules:
  0.0 325.9 jit_solution(4094946442630826706)
XLA Ops:
  6.5 0.7 all-gather.5.cloned.1.call-update
  7.3 1.6 tile.2
  8.9 10.5 %all-to-all-start = ((bf16[32,128,64]{1,2,0:T(8,128)(2,1)}), bf16[32,128,64]{1,2,0:T(8,128)(2,1)S(1)}, u32[]{:S(2)}, u32[]{:S(2)}) async-start(bf16[32,128,64]{1,2,0:T(8,128)(2,1)} %tile.2), calls=%async_computation | async-start | bytes 1048576 | tf_op jit(solution)/shard_map/all_to_all | solution.py:17
  19.5 0.8 reduce-window.8
  20.4 0.7 compare_bitcast_fusion
  21.0 12.7 %all-to-all-done = bf16[32,128,64]{1,2,0:T(8,128)(2,1)S(1)} async-done(((bf16[32,128,64]{1,2,0:T(8,128)(2,1)}), bf16[32,128,64]{1,2,0:T(8,128)(2,1)S(1)}, u32[]{:S(2)}, u32[]{:S(2)}) %all-to-all-start) | async-done | bytes 524320 | tf_op jit(solution)/shard_map/all_to_all | solution.py:17
  33.7 0.5 fusion.2
  34.2 61.4 %all-gather.5.cloned.1.call-done = bf16[32,448,64]{1,2,0:T(8,128)(2,1)} async-done(((bf16[1,448,64]{1,2,0:T(8,128)(2,1)}), bf16[32,448,64]{1,2,0:T(8,128)(2,1)}) %all-gather.5.cloned.1.call-update) | async-done | bytes 1835024 | tf_op jit(solution)/shard_map/all_gather | solution.py:32
  95.6 2.8 copy.27
  98.3 3.4 %reshape.120 = bf16[14336,64]{0,1:T(8,128)(2,1)} reshape(bf16[32,448,64]{1,0,2:T(8,128)(2,1)S(1)} %copy.27) | data formatting | bytes 3670016
  101.7 4.0 %fusion = f32[128,64]{0,1:T(8,128)S(1)} fusion(bf16[14336,64]{0,1:T(8,128)(2,1)} %reshape.120, bf16[1,128,14336]{2,1,0:T(8,128)(2,1)} %param.9), kind=kOutput, calls=%fused_computation | convolution fusion | flops 234881024 | bytes 5537792 | tf_op jit(solution)/shard_map/dot_general | solution.py:30
  105.7 0.3 fusion.17
  106.0 0.7 reshape.118
  106.8 147.6 %all-reduce.2.cloned.1.call-done = f32[4,4096]{1,0:T(4,128)} async-done(((f32[4,4096]{1,0:T(4,128)}), f32[4,4096]{1,0:T(4,128)}) %all-reduce.2.cloned.1.call-update) | async-done | bytes 65552 | tf_op jit(solution)/shard_map/psum | solution.py:45
  254.5 47.1 %all-gather.7.cloned.1.call-done = f32[16,4,4096]{2,1,0:T(4,128)} async-done(((f32[1,4,4096]{2,1,0:T(4,128)}), f32[16,4,4096]{2,1,0:T(4,128)}) %all-gather.7.cloned.1.call-update) | async-done | bytes 1048592 | tf_op jit(solution)/shard_map/all_gather | solution.py:46
  301.6 1.6 reshape.122
  303.2 1.6 select_reduce_fusion.1
  305.6 5.8 %cholesky.17 = f32[64,64]{1,0:T(8,128)S(1)} custom-call(f32[64,64]{1,0:T(8,128)S(1)} %fusion.12), custom_call_target="Cholesky" | custom-call | tf_op jit(solution)/shard_map/jit(cholesky)/cholesky | solution.py:51
  311.5 0.6 compare_reduce_fusion
  312.1 0.7 fusion.6
  312.8 4.9 %custom-call.8 = f32[1,64,64]{1,2,0:T(8,128)S(1)} custom-call(f32[1,64,64]{2,1,0:T(8,128)S(1)} %fusion.6), custom_call_target="InvertDiagBlocksLowerTriangular" | custom-call | tf_op jit(solution)/shard_map/triangular_solve | solution.py:53
  317.7 0.6 fusion.18
  318.5 0.2 fusion.7
  318.7 0.8 fusion.13
  (21 shorter events, 0.6 us)
Async XLA Ops:
  6.5 27.2 %copy-start = (bf16[1,128,4096]{2,1,0:T(8,128)(2,1)S(1)}, bf16[1,128,4096]{2,1,0:T(8,128)(2,1)}, u32[]{:S(2)}) copy-start(bf16[1,128,4096]{2,1,0:T(8,128)(2,1)} %param.8) | copy-start | bytes 3145732
  6.5 89.1 %all-gather.5.cloned.1.call-start = ((), (), s32[]{:S(2)}) async-start(), calls=%async_computation.2 | async-start | bytes 2162688 | tf_op jit(solution)/shard_map/all_gather | solution.py:32
  8.9 24.8 %all-to-all-start = ((bf16[32,128,64]{1,2,0:T(8,128)(2,1)}), bf16[32,128,64]{1,2,0:T(8,128)(2,1)S(1)}, u32[]{:S(2)}, u32[]{:S(2)}) async-start(bf16[32,128,64]{1,2,0:T(8,128)(2,1)} %tile.2), calls=%async_computation | async-start | bytes 1048576 | tf_op jit(solution)/shard_map/all_to_all | solution.py:17
  19.4 235.0 %all-reduce.2.cloned.1.call-start = ((), (), s32[]{:S(2)}) async-start(), calls=%async_computation.1 | async-start | bytes 131072 | tf_op jit(solution)/shard_map/psum | solution.py:45
  106.8 194.8 %all-gather.7.cloned.1.call-start = ((), (), s32[]{:S(2)}) async-start(), calls=%async_computation.3 | async-start | bytes 1114112 | tf_op jit(solution)/shard_map/all_gather | solution.py:46
  254.5 63.2 %copy-start.1 = (bf16[32,4096]{1,0:T(8,128)(2,1)S(1)}, bf16[32,4096]{1,0:T(8,128)(2,1)}, u32[]{:S(2)}) copy-start(bf16[32,4096]{1,0:T(8,128)(2,1)} %param.15) | copy-start | bytes 786436
  303.2 15.5 %copy-start.2 = (s32[64]{0:T(128)S(1)}, s32[64]{0:T(128)}, u32[]{:S(2)}) copy-start(s32[64]{0:T(128)} %param.12) | copy-start | bytes 772
Sparse Core Ops, SparseCore 0:
  10.5 85.0 all-gather.4
  106.9 147.5 all-reduce.1
  256.6 44.9 all-gather.6

commit v2 on v0

--- a/solution.py
+++ b/solution.py
@@ -35,7 +35,7 @@
     weighted = (onehot[:, :, None] * pg[:, None, :]).reshape(slots, DOC_GRP * PROJ_OUT)
     partial_grads = jnp.dot(weighted.T, px, precision=lax.Precision.HIGHEST).reshape(DOC_GRP, FEAT)
     ndocs = DOC_GRP * lax.axis_size("dp")
-    group_grads = lax.psum(partial_grads, "seq")
+    group_grads = lax.all_gather(partial_grads, "seq").sum(axis=0)
     doc_grads = lax.all_gather(group_grads, "dp", axis=0, tiled=True)
     gram = jnp.dot(doc_grads, doc_grads.T, precision=lax.Precision.HIGHEST)
     cross = jnp.dot(doc_grads, test_grads.astype(jnp.float32).T, precision=lax.Precision.HIGHEST)

time: 326 us -> 259 us (0.79)
  waiting for transfers between devices: 240 us -> 170 us
    psum x1 -> x0, waiting for transfers between devices: 148 us -> none  [per_device(): group_grads = lax.psum(partial_grads, 'seq')]
    all_gather x0 -> x1, waiting for transfers between devices: none -> 80.9 us  [per_device(): group_grads = lax.all_gather(partial_grads, 'seq').sum(axis=0)]
    all_gather x1, waiting for transfers between devices: 47.1 us -> 43.7 us  [per_device(): doc_grads = lax.all_gather(group_grads, 'dp', axis=0, tiled=True)]
where the time goes in v2:
time: 259 us; the launch traced here: 258 us
  waiting for transfers between devices  170 us (66%)
  blocking collectives  41.4 us (16%)
  other arithmetic  16.2 us (6%)
  between operations  13.9 us (5%)
  local copies, waits for them, and re-layouts  8.61 us (3%)
  matrix products  8 us (3%)
    all_gather x1, waiting for transfers between devices, per_device(): group_grads = lax.all_gather(partial_grads, 'seq').sum(axis=0)  80.9 us
    all_gather x1, waiting for transfers between devices, per_device(): lax.all_gather(proj_out, 'seq', axis=0, tiled=True)  44.7 us
    all_gather x1, waiting for transfers between devices, per_device(): doc_grads = lax.all_gather(group_grads, 'dp', axis=0, tiled=True)  43.7 us
    all_gather x1, blocking collectives, per_device(): lax.all_gather(proj_in, 'seq', axis=0, tiled=True)  41.4 us
    another operation x3, other arithmetic, per_device(): factor = jnp.linalg.cholesky(matrix)  6.52 us
    another operation x2, other arithmetic, per_device(): lax.linalg.triangular_solve(factor, middle, left_side=True, lower=True, t...  5.55 us
  transfers between devices with their start and end apart: 3, of which 3 were waited for; matrix products, arithmetic and copies ran while one was open for 1% of the time, Pallas kernels for 0%

profile of v2, /device:TPU:1, one launch (start us, length us, event | category | flops | bytes accessed | tf_op | source)
XLA Modules:
  0.0 258.3 jit_solution(12958160068024231276)
XLA Ops:
  6.5 0.7 all-gather.8.cloned.1.call-update
  7.3 0.8 reduce-window.8
  8.2 41.4 %all_gather.13 = bf16[4096,64]{0,1:T(8,128)(2,1)S(1)} all-gather(bf16[128,64]{0,1:T(8,128)(2,1)} %param.13), channel_id=1, replica_groups=mesh['dp'=16,'seq'=32] {'seq'}, dimensions={0}, use_global_device_ids=true | all-gather | bytes 540672 | tf_op jit(solution)/shard_map/all_gather | solution.py:19
  49.6 0.7 compare_bitcast_fusion
  50.3 0.5 fusion.2
  50.8 44.7 %all-gather.8.cloned.1.call-done = bf16[32,448,64]{1,2,0:T(8,128)(2,1)} async-done(((bf16[1,448,64]{1,2,0:T(8,128)(2,1)}), bf16[32,448,64]{1,2,0:T(8,128)(2,1)}) %all-gather.8.cloned.1.call-update) | async-done | bytes 1835024 | tf_op jit(solution)/shard_map/all_gather | solution.py:25
  95.6 2.8 %copy.20 = bf16[32,448,64]{1,0,2:T(8,128)(2,1)S(1)} copy(bf16[32,448,64]{1,2,0:T(8,128)(2,1)} %all-gather.8.cloned.1.call-done) | data formatting | bytes 3670016 | tf_op jit(solution)/shard_map/all_gather | solution.py:25
  98.3 3.4 %reshape.109 = bf16[14336,64]{0,1:T(8,128)(2,1)} reshape(bf16[32,448,64]{1,0,2:T(8,128)(2,1)S(1)} %copy.20) | data formatting | bytes 3670016
  101.7 4.0 %fusion = f32[128,64]{0,1:T(8,128)S(1)} fusion(bf16[14336,64]{0,1:T(8,128)(2,1)} %reshape.109, bf16[1,128,14336]{2,1,0:T(8,128)(2,1)} %param.9), kind=kOutput, calls=%fused_computation | convolution fusion | flops 234881024 | bytes 5537792 | tf_op jit(solution)/shard_map/dot_general | solution.py:23
  105.7 0.3 fusion.15
  106.0 0.7 all_gather_reshape.3
  106.8 80.9 %all-gather.6.cloned.1.call-done = f32[32,4,4096]{2,1,0:T(4,128)} async-done(((f32[1,4,4096]{2,1,0:T(4,128)}), f32[32,4,4096]{2,1,0:T(4,128)}) %all-gather.6.cloned.1.call-update) | async-done | bytes 2097168 | tf_op jit(solution)/shard_map/all_gather | solution.py:38
  187.6 2.5 reduce_sum.29
  190.2 43.7 %all-gather.10.cloned.1.call-done = f32[16,4,4096]{2,1,0:T(4,128)} async-done(((f32[1,4,4096]{2,1,0:T(4,128)}), f32[16,4,4096]{2,1,0:T(4,128)}) %all-gather.10.cloned.1.call-update) | async-done | bytes 1048592 | tf_op jit(solution)/shard_map/all_gather | solution.py:39
  233.9 1.6 reshape.111
  235.5 1.6 select_reduce_fusion.1
  237.9 5.8 %cholesky.17 = f32[64,64]{1,0:T(8,128)S(1)} custom-call(f32[64,64]{1,0:T(8,128)S(1)} %fusion.10), custom_call_target="Cholesky" | custom-call | tf_op jit(solution)/shard_map/jit(cholesky)/cholesky | solution.py:44
  243.8 0.6 compare_reduce_fusion
  244.4 0.7 fusion.4
  245.1 4.9 %custom-call.8 = f32[1,64,64]{1,2,0:T(8,128)S(1)} custom-call(f32[1,64,64]{2,1,0:T(8,128)S(1)} %fusion.4), custom_call_target="InvertDiagBlocksLowerTriangular" | custom-call | tf_op jit(solution)/shard_map/triangular_solve | solution.py:46
  250.0 0.6 fusion.16
  250.6 0.1 fusion.7
  250.8 0.2 fusion.5
  251.0 0.8 fusion.11
  (20 shorter events, 0.5 us)
Async XLA Ops:
  6.5 43.8 %copy-start = (bf16[1,128,4096]{2,1,0:T(8,128)(2,1)S(1)}, bf16[1,128,4096]{2,1,0:T(8,128)(2,1)}, u32[]{:S(2)}) copy-start(bf16[1,128,4096]{2,1,0:T(8,128)(2,1)} %param.8) | copy-start | bytes 3145732
  6.5 89.0 %all-gather.8.cloned.1.call-start = ((), (), s32[]{:S(2)}) async-start(), calls=%async_computation.1 | async-start | bytes 2162688 | tf_op jit(solution)/shard_map/all_gather | solution.py:25
  7.3 180.4 %all-gather.6.cloned.1.call-start = ((), (), s32[]{:S(2)}) async-start(), calls=%async_computation | async-start | bytes 2162688 | tf_op jit(solution)/shard_map/all_gather | solution.py:38
  106.7 127.2 %all-gather.10.cloned.1.call-start = ((), (), s32[]{:S(2)}) async-start(), calls=%async_computation.2 | async-start | bytes 1114112 | tf_op jit(solution)/shard_map/all_gather | solution.py:39
  190.2 59.8 %copy-start.1 = (bf16[32,4096]{1,0:T(8,128)(2,1)S(1)}, bf16[32,4096]{1,0:T(8,128)(2,1)}, u32[]{:S(2)}) copy-start(bf16[32,4096]{1,0:T(8,128)(2,1)} %param.15) | copy-start | bytes 786436
  235.5 15.5 %copy-start.2 = (s32[64]{0:T(128)S(1)}, s32[64]{0:T(128)}, u32[]{:S(2)}) copy-start(s32[64]{0:T(128)} %param.12) | copy-start | bytes 772
Sparse Core Ops, SparseCore 0:
  10.5 84.9 all-gather.7
  106.8 80.7 all-gather.5
  190.3 43.5 all-gather.9
